TPU v7x, 32 devices: a whole 2x2x4 slice. The times are simulated.
32 devices in a mesh: parts: 2 (over y), wide: 4 (over z), narrow: 4 (over x, core).
Axes of the slice: x: 2, y: 2, z: 4, core: 2. Of those that a mesh axis runs over, the one named last changes fastest.
Arguments:
- teacher: bfloat16 [4096, 4096], P(('parts', 'wide', 'narrow')), parts along dimension 0, may hold values from -6 to 6
- weight: float32 [4096, 256], replicated, may hold values from -0.09375 to 0.09375
- block_mask: int32 [8, 4], P('parts'), parts along dimension 0, may hold values 0 or 1
- item_group: int32 [4096], P(('parts', 'wide', 'narrow')), parts along dimension 0, may hold values from 0 to 7
Outputs:
- grad_weight: float32 [8192, 256], P(('parts', 'wide', 'narrow')), parts along dimension 0
There are 2 independent parts, one for each index of `parts`. A program takes and returns all parts, laid end to end along the dimension named above; an argument that names none is the same for every part. Nothing has to cross between parts.
Inputs may be any that keep to these rules, and one draw needn't show every extreme that they name: `block_mask`: 0 or 1 for each ordered pair of blocks.
All inputs are finite; a program needn't handle non-finite values.
Results may differ from a plain program's by a relative error of at most 0.0083.
Values may be sent and summed in bfloat16 or wider, within the bound.
A program may use at most 64 MiB of HBM per device.

v0:
```python
import jax
import jax.numpy as jnp
from jax import lax
from jax.sharding import PartitionSpec as P


def shifted(value, axis, steps):
    count = lax.axis_size(axis)
    pairs = [(source, (source + steps) % count) for source in range(count)]
    return lax.ppermute(value, axis, pairs)


def tile_terms(panel, piece, factor):
    panel_t, panel_s, panel_g = panel
    piece_t, piece_s, piece_g = piece
    teach = (
        lax.dot_general(
            panel_t, piece_t, (((1,), (1,)), ((), ())), preferred_element_type=jnp.float32
        )
        / panel_t.shape[1]
    )
    stud = (
        lax.dot_general(
            panel_s, piece_s, (((1,), (1,)), ((), ())), preferred_element_type=jnp.float32
        )
        / panel_s.shape[1]
    )
    same = (panel_g[:, None] == piece_g[None, :]).astype(jnp.float32)
    pair_term = (factor * (1.0 + same) * (stud - teach)).astype(jnp.bfloat16)
    to_panel = jnp.dot(pair_term, piece_s, preferred_element_type=jnp.float32)
    to_piece = lax.dot_general(
        pair_term, panel_s, (((0,), (0,)), ((), ())), preferred_element_type=jnp.float32
    )
    return (to_panel, to_piece)


def per_device(teacher, weight, block_mask, item_group):
    rows_here = teacher.shape[0]
    width_out = weight.shape[1]
    low_weight = weight.astype(jnp.bfloat16)
    own_student = jnp.dot(teacher, low_weight, preferred_element_type=jnp.float32).astype(
        jnp.bfloat16
    )
    own_group = item_group.astype(jnp.bfloat16)
    panel = (
        lax.all_gather(teacher, "narrow", axis=0, tiled=True),
        lax.all_gather(own_student, "narrow", axis=0, tiled=True),
        lax.all_gather(own_group, "narrow", axis=0, tiled=True),
    )
    wide_count = lax.axis_size("wide")
    narrow_count = lax.axis_size("narrow")
    half_loop = wide_count // 2
    here = lax.axis_index("wide")
    mask_float = block_mask.astype(jnp.float32)
    row_ids = lax.broadcasted_iota(jnp.int32, mask_float.shape, 0)
    col_ids = lax.broadcasted_iota(jnp.int32, mask_float.shape, 1)

    def pick_mask(first, second):
        return jnp.sum(jnp.where((row_ids == first) & (col_ids == second), mask_float, 0.0))

    def tile_factor(step):
        other = (here - step) % wide_count
        forward = pick_mask(here, other)
        backward = pick_mask(other, here)
        both_ways = (step > 0) & (step < half_loop)
        return forward + jnp.where(both_ways, backward, 0.0)

    moving = (teacher, own_student, own_group)

    def advance(carried):
        return shifted((carried[0], carried[1], carried[2]), "wide", 1)

    def run_tile(carried, step):
        factor = tile_factor(step)
        return tile_terms(panel, carried, factor)

    panel_sum, accum = run_tile(moving, jnp.int32(0))

    def step_body(step, carry):
        carried, accum, panel_sum = carry
        carried = advance(carried)
        accum = shifted(accum, "wide", 1)
        to_panel, to_piece = run_tile(carried, step)
        return (carried, accum + to_piece, panel_sum + to_panel)

    moving, accum, panel_sum = lax.fori_loop(
        1, half_loop + 1, step_body, (moving, accum, panel_sum)
    )
    returned = shifted(accum, "wide", -half_loop)
    owned = lax.psum_scatter(panel_sum, "narrow", scatter_dimension=0, tiled=True)
    total_items = rows_here * wide_count * narrow_count
    coef = 2.0 * teacher.shape[1] / (total_items * width_out)
    grad_student = ((owned + returned) * coef).astype(jnp.bfloat16)
    return lax.psum_scatter(
        lax.dot_general(
            teacher, grad_student, (((0,), (0,)), ((), ())), preferred_element_type=jnp.float32
        ),
        ("wide", "narrow"),
        scatter_dimension=0,
        tiled=True,
    )


def solution(mesh):
    in_specs = (
        P(("parts", "wide", "narrow"), None),
        P(),
        P("parts", None),
        P(("parts", "wide", "narrow")),
    )
    out_specs = P(("parts", "wide", "narrow"), None)
    return jax.shard_map(
        per_device, mesh=mesh, in_specs=in_specs, out_specs=out_specs, check_vma=False
    )
```

profile of v0, /device:TPU:0, one launch (start us, length us, event | category | flops | bytes accessed | tf_op | source)
XLA Modules:
  0.0 225.8 jit_solution(6743651973957401759)
XLA Ops:
  6.5 0.0 copy-start
  6.5 0.0 copy-start.2
  6.5 0.0 all-gather.3.cloned.1.call-start
  6.5 0.7 all-gather.3.cloned.1.call-update
  7.3 0.0 reduce-scatter.3.cloned.1.call-start
  7.3 2.3 %copy.9 = bf16[128,4096]{1,0:T(8,128)(2,1)} copy(bf16[128,4096]{1,0:T(8,128)(2,1)} %param.6) | data formatting | bytes 2097152
  9.6 0.7 convert_element_type.44
  10.3 0.7 convert_bitcast_fusion
  10.9 5.9 %all-gather = bf16[4,1,128]{2,1,0:T(2,128)(2,1)S(1)} all-gather(bf16[1,1,128]{2,1,0:T(2,128)(2,1)S(1)} %get-tuple-element.405), channel_id=1, replica_groups=mesh['parts'=2,'wide'=4,'narrow'=4] {'narrow'}, dimensions={0}, use_global_device_ids=true | all-gather | bytes 1280 | tf_op jit(solution)/shard_map/all_gather | solution.py:48
  16.9 3.5 %fusion.12 = bf16[128,256]{1,0:T(8,128)(2,1)S(1)} fusion(bf16[128,4096]{1,0:T(8,128)(2,1)} %param.6, f32[4096,256]{1,0:T(8,128)} %param.7), kind=kOutput, calls=%fused_computation.24 | convolution fusion | flops 269516800 | bytes 5308416 | tf_op jit(solution)/shard_map/dot_general | solution.py:41
  20.4 7.9 %all_gather.10 = bf16[512,256]{1,0:T(8,128)(2,1)S(1)} all-gather(bf16[128,256]{1,0:T(8,128)(2,1)S(1)} %fusion.12), channel_id=1, replica_groups=mesh['parts'=2,'wide'=4,'narrow'=4] {'narrow'}, dimensions={0}, use_global_device_ids=true | all-gather | bytes 327680 | tf_op jit(solution)/shard_map/all_gather | solution.py:47
  28.3 0.0 copy-done.2
  28.3 0.7 select_reduce_fusion.2
  29.0 18.5 %all-gather.3.cloned.1.call-done = bf16[512,4096]{1,0:T(8,128)(2,1)} async-done(((bf16[128,4096]{1,0:T(8,128)(2,1)}), bf16[512,4096]{1,0:T(8,128)(2,1)}) %all-gather.3.cloned.1.call-update) | async-done | bytes 4194320 | tf_op jit(solution)/shard_map/all_gather | solution.py:46
  47.5 0.0 copy-done
  47.5 3.4 %convolution_multiply_fusion.3 = f32[512,128]{1,0:T(8,128)S(1)} fusion(bf16[512,4096]{1,0:T(8,128)(2,1)} %all-gather.3.cloned.1.call-done, bf16[128,4096]{1,0:T(8,128)(2,1)S(1)} %copy-done), kind=kOutput, calls=%fused_computation.22 | convolution fusion | flops 536936448 | bytes 5505024 | tf_op jit(solution)/shard_map/dot_general | solution.py:17
  51.0 0.9 fusion.11
  51.8 0.2 fusion.17
  52.1 0.2 fusion.18
  52.3 68.4 %while.25 = (s32[]{:T(128)}, bf16[128,4096]{1,0:T(8,128)(2,1)}, bf16[128,256]{1,0:T(8,128)(2,1)S(1)}, bf16[128]{0:T(256)(128)(2,1)S(1)}, f32[128,256]{1,0:T(8,12...) while((s32[]{:T(128)}, bf16[128,4096]{1,0:T(8,128)(2,1)}, ...), condition=%wide.region_4.5_spmd.clone.clone, body=%wide.region_1.4_spmd.clone.clone.sunk | while | flops 638288000 | bytes 15338808 | solution.py:86
  52.3 1.5 collective-permute-start
  53.8 1.5 collective-permute-start.2
  55.3 1.5 collective-permute-start.1
  56.8 0.5 collective-permute-start.3
  57.3 0.6 select_reduce_fusion.4
  59.1 21.3 %collective-permute-done.2 = bf16[128]{0:T(256)(128)(2,1)S(1)} collective-permute-done((bf16[128]{0:T(256)(128)(2,1)S(1)}, bf16[128]{0:T(256)(128)(2,1)S(1)}, u32[]{:S(2)}, u32[]{:S(2)}) %collective-permute-start.2) | collective-permute-done | bytes 288 | tf_op jit(solution)/shard_map/while/body/eval_jaxpr/ppermute | solution.py:10
  80.4 1.3 collective-permute-done.1
  81.8 0.0 collective-permute-done
  81.8 1.0 copy.21
  82.8 3.4 %convolution_multiply_fusion.5 = f32[512,128]{1,0:T(8,128)S(1)} fusion(bf16[512,4096]{1,0:T(8,128)(2,1)} %get-tuple-element.524, bf16[128,4096]{1,0:T(8,128)(2,1)S(1)} %collective-permute-done), kind=kOutput, calls=%fused_computation.5.clone.1 | convolution fusion | flops 536936448 | bytes 5505024 | tf_op jit(solution)/shard_map/while/body/eval_jaxpr/dot_general | solution.py:17
  86.2 0.2 multiply_convert_fusion.4
  86.4 0.0 collective-permute-done.3
  86.5 0.2 convolution_add_fusion.4
  86.7 0.2 convolution_add_fusion.5
  86.9 0.1 collective-permute-start
  87.0 1.1 collective-permute-start.2
  88.1 1.5 collective-permute-start.1
  89.6 2.3 %collective-permute-start.3 = (f32[128,256]{1,0:T(8,128)S(1)}, f32[128,256]{1,0:T(8,128)S(1)}, u32[]{:S(2)}, u32[]{:S(2)}) collective-permute-start(f32[128,256]{1,0:T(8,128)S(1)} %get-tuple-element.501), channel_id=1, source_target_pairs={{0,4},{4,8},{8,12},{12,0},{1,5},{5,9},{9,13},{13,1},{2,6},{6,10},{... | collective-permute-start | bytes 393224 | tf_op jit(solution)/shard_map/while/body/eval_jaxpr/ppermute | solution.py:10
  91.9 0.6 select_reduce_fusion.4
  93.7 21.2 %collective-permute-done.2 = bf16[128]{0:T(256)(128)(2,1)S(1)} collective-permute-done((bf16[128]{0:T(256)(128)(2,1)S(1)}, bf16[128]{0:T(256)(128)(2,1)S(1)}, u32[]{:S(2)}, u32[]{:S(2)}) %collective-permute-start.2) | collective-permute-done | bytes 288 | tf_op jit(solution)/shard_map/while/body/eval_jaxpr/ppermute | solution.py:10
  114.9 0.6 collective-permute-done.1
  115.6 0.0 collective-permute-done
  115.6 1.0 copy.21
  116.6 3.4 %convolution_multiply_fusion.5 = f32[512,128]{1,0:T(8,128)S(1)} fusion(bf16[512,4096]{1,0:T(8,128)(2,1)} %get-tuple-element.524, bf16[128,4096]{1,0:T(8,128)(2,1)S(1)} %collective-permute-done), kind=kOutput, calls=%fused_computation.5.clone.1 | convolution fusion | flops 536936448 | bytes 5505024 | tf_op jit(solution)/shard_map/while/body/eval_jaxpr/dot_general | solution.py:17
  120.0 0.2 multiply_convert_fusion.4
  120.2 0.0 collective-permute-done.3
  120.3 0.2 convolution_add_fusion.4
  120.5 0.2 convolution_add_fusion.5
  120.7 0.0 copy-start.1
  120.7 0.8 copy-done.1
  121.5 0.0 reduce-scatter.3.cloned.1.call-update
  121.5 0.0 reduce-scatter.5.cloned.1.call-start
  121.6 0.1 collective-permute-start.4
  121.7 5.9 %collective-permute-done.4 = f32[128,256]{1,0:T(8,128)S(1)} collective-permute-done((f32[128,256]{1,0:T(8,128)S(1)}, f32[128,256]{1,0:T(8,128)S(1)}, u32[]{:S(2)}, u32[]{:S(2)}) %collective-permute-start.4) | collective-permute-done | bytes 131104 | tf_op jit(solution)/shard_map/ppermute | solution.py:10
  127.5 13.1 %reduce-scatter.3.cloned.1.call-done = f32[128,256]{1,0:T(8,128)} async-done(((f32[512,256]{1,0:T(8,128)}), f32[128,256]{1,0:T(8,128)}) %reduce-scatter.3.cloned.1.call-update) | async-done | bytes 131088 | tf_op jit(solution)/shard_map/reduce_scatter | solution.py:90
  140.6 3.6 %convolution_bitcast_fusion = f32[4096,256]{0,1:T(8,128)} fusion(bf16[128,4096]{1,0:T(8,128)(2,1)S(1)} %copy-done, f32[128,256]{1,0:T(8,128)} %reduce-scatter.3.cloned.1.call-done, f32[128,256]{1,0:T(8,128)S(1)} %collective-permute-done.4), kind=kOutput, calls=%fused_computation.16 | convolution fusion | flops 268533760 | bytes 5505024 | tf_op jit(solution)/shard_map/dot_general | solution.py:95
  144.2 0.0 reduce-scatter.5.cloned.1.call-update
  144.2 73.2 %reduce-scatter.5.cloned.1.call-done = f32[256,256]{0,1:T(8,128)} async-done(((f32[4096,256]{0,1:T(8,128)}), f32[256,256]{0,1:T(8,128)}) %reduce-scatter.5.cloned.1.call-update) | async-done | bytes 262160 | tf_op jit(solution)/shard_map/reduce_scatter | solution.py:94
  217.5 1.8 copy.7
  (6 shorter events, 0.0 us)
Async XLA Ops:
  6.5 41.0 %copy-start = (bf16[128,4096]{1,0:T(8,128)(2,1)S(1)}, bf16[128,4096]{1,0:T(8,128)(2,1)}, u32[]{:S(2)}) copy-start(bf16[128,4096]{1,0:T(8,128)(2,1)} %param.6) | copy-start | bytes 3145732
  6.5 21.8 %copy-start.2 = (s32[4,4]{1,0:T(4,128)S(1)}, s32[4,4]{1,0:T(4,128)}, u32[]{:S(2)}) copy-start(s32[4,4]{1,0:T(4,128)} %param.8) | copy-start | bytes 196
  6.5 41.0 %all-gather.3.cloned.1.call-start = ((), (), s32[]{:S(2)}) async-start(), calls=%async_computation.2 | async-start | bytes 5242880 | tf_op jit(solution)/shard_map/all_gather | solution.py:46
  7.3 133.4 %reduce-scatter.3.cloned.1.call-start = ((), (), s32[]{:S(2)}) async-start(), calls=%async_computation.3 | async-start | bytes 655360 | tf_op jit(solution)/shard_map/reduce_scatter | solution.py:90
  52.3 29.5 %collective-permute-start = (bf16[128,4096]{1,0:T(8,128)(2,1)}, bf16[128,4096]{1,0:T(8,128)(2,1)S(1)}, u32[]{:S(2)}, u32[]{:S(2)}) collective-permute-start(bf16[128,4096]{1,0:T(8,128)(2,1)} %get-tuple-element.498), channel_id=1, source_target_pairs={{0,4},{4,8},{8,12},{12,0},{1,5},{5,9},{9,13},{13,1},{2,6},{6,10},{... | collective-permute-start | bytes 3145736 | tf_op jit(solution)/shard_map/while/body/eval_jaxpr/ppermute | solution.py:10
  53.8 26.6 %collective-permute-start.2 = (bf16[128]{0:T(256)(128)(2,1)S(1)}, bf16[128]{0:T(256)(128)(2,1)S(1)}, u32[]{:S(2)}, u32[]{:S(2)}) collective-permute-start(bf16[128]{0:T(256)(128)(2,1)S(1)} %get-tuple-element.500), channel_id=1, source_target_pairs={{0,4},{4,8},{8,12},{12,0},{1,5},{5,9},{9,13},{13,1},{2,6},{6,10},{... | collective-permute-start | bytes 776 | tf_op jit(solution)/shard_map/while/body/eval_jaxpr/ppermute | solution.py:10
  55.3 26.5 %collective-permute-start.1 = (bf16[128,256]{1,0:T(8,128)(2,1)S(1)}, bf16[128,256]{1,0:T(8,128)(2,1)S(1)}, u32[]{:S(2)}, u32[]{:S(2)}) collective-permute-start(bf16[128,256]{1,0:T(8,128)(2,1)S(1)} %get-tuple-element.499), channel_id=1, source_target_pairs={{0,4},{4,8},{8,12},{12,0},{1,5},{5,9},{9,13},{13,1},{2,6},{6,10},{... | collective-permute-start | bytes 196616 | tf_op jit(solution)/shard_map/while/body/eval_jaxpr/ppermute | solution.py:10
  56.8 29.6 %collective-permute-start.3 = (f32[128,256]{1,0:T(8,128)S(1)}, f32[128,256]{1,0:T(8,128)S(1)}, u32[]{:S(2)}, u32[]{:S(2)}) collective-permute-start(f32[128,256]{1,0:T(8,128)S(1)} %get-tuple-element.501), channel_id=1, source_target_pairs={{0,4},{4,8},{8,12},{12,0},{1,5},{5,9},{9,13},{13,1},{2,6},{6,10},{... | collective-permute-start | bytes 393224 | tf_op jit(solution)/shard_map/while/body/eval_jaxpr/ppermute | solution.py:10
  86.9 28.7 %collective-permute-start = (bf16[128,4096]{1,0:T(8,128)(2,1)}, bf16[128,4096]{1,0:T(8,128)(2,1)S(1)}, u32[]{:S(2)}, u32[]{:S(2)}) collective-permute-start(bf16[128,4096]{1,0:T(8,128)(2,1)} %get-tuple-element.498), channel_id=1, source_target_pairs={{0,4},{4,8},{8,12},{12,0},{1,5},{5,9},{9,13},{13,1},{2,6},{6,10},{... | collective-permute-start | bytes 3145736 | tf_op jit(solution)/shard_map/while/body/eval_jaxpr/ppermute | solution.py:10
  87.0 27.9 %collective-permute-start.2 = (bf16[128]{0:T(256)(128)(2,1)S(1)}, bf16[128]{0:T(256)(128)(2,1)S(1)}, u32[]{:S(2)}, u32[]{:S(2)}) collective-permute-start(bf16[128]{0:T(256)(128)(2,1)S(1)} %get-tuple-element.500), channel_id=1, source_target_pairs={{0,4},{4,8},{8,12},{12,0},{1,5},{5,9},{9,13},{13,1},{2,6},{6,10},{... | collective-permute-start | bytes 776 | tf_op jit(solution)/shard_map/while/body/eval_jaxpr/ppermute | solution.py:10
  88.1 27.4 %collective-permute-start.1 = (bf16[128,256]{1,0:T(8,128)(2,1)S(1)}, bf16[128,256]{1,0:T(8,128)(2,1)S(1)}, u32[]{:S(2)}, u32[]{:S(2)}) collective-permute-start(bf16[128,256]{1,0:T(8,128)(2,1)S(1)} %get-tuple-element.499), channel_id=1, source_target_pairs={{0,4},{4,8},{8,12},{12,0},{1,5},{5,9},{9,13},{13,1},{2,6},{6,10},{... | collective-permute-start | bytes 196616 | tf_op jit(solution)/shard_map/while/body/eval_jaxpr/ppermute | solution.py:10
  89.6 30.6 %collective-permute-start.3 = (f32[128,256]{1,0:T(8,128)S(1)}, f32[128,256]{1,0:T(8,128)S(1)}, u32[]{:S(2)}, u32[]{:S(2)}) collective-permute-start(f32[128,256]{1,0:T(8,128)S(1)} %get-tuple-element.501), channel_id=1, source_target_pairs={{0,4},{4,8},{8,12},{12,0},{1,5},{5,9},{9,13},{13,1},{2,6},{6,10},{... | collective-permute-start | bytes 393224 | tf_op jit(solution)/shard_map/while/body/eval_jaxpr/ppermute | solution.py:10
  120.7 0.8 copy-start.1
  121.5 95.9 %reduce-scatter.5.cloned.1.call-start = ((), (), s32[]{:S(2)}) async-start(), calls=%async_computation.4 | async-start | bytes 4456448 | tf_op jit(solution)/shard_map/reduce_scatter | solution.py:94
  121.6 5.9 %collective-permute-start.4 = (f32[128,256]{1,0:T(8,128)S(1)}, f32[128,256]{1,0:T(8,128)S(1)}, u32[]{:S(2)}, u32[]{:S(2)}) collective-permute-start(f32[128,256]{1,0:T(8,128)S(1)} %get-tuple-element.322), channel_id=1, source_target_pairs={{0,8},{4,12},{8,0},{12,4},{1,9},{5,13},{9,1},{13,5},{2,10},{6,14},... | collective-permute-start | bytes 393224 | tf_op jit(solution)/shard_map/ppermute | solution.py:10
Sparse Core Ops, SparseCore 0:
  8.9 38.5 all-gather.2
  121.7 18.9 reduce-scatter.2
  145.0 72.4 reduce-scatter.4
where the time goes:
time: 226 us
  waiting for transfers between devices  156 us (69%)
  matrix products  20 us (9%)
  blocking collectives  13.9 us (6%)
  between operations  13.2 us (6%)
  starting transfers between devices  10.2 us (5%)
  local copies, waits for them, and re-layouts  6.83 us (3%)
  other arithmetic  3.27 us (1%)
  loops' own time  2.5 us (1%)
    reduce_scatter x1, waiting for transfers between devices, per_device(): lax.psum_scatter(lax.dot_general(teacher, grad_student, (((0,), (0,)), ((...  73.2 us
    ppermute x9, waiting for transfers between devices, shifted(): return lax.ppermute(value, axis, pairs)  50.3 us
    all_gather x1, waiting for transfers between devices, per_device(): lax.all_gather(teacher, 'narrow', axis=0, tiled=True)  18.5 us
    reduce_scatter x1, waiting for transfers between devices, per_device(): lax.psum_scatter(panel_sum, 'narrow', scatter_dimension=0, tiled=True)  13.1 us
    dot_general x3, matrix products, tile_terms(): lax.dot_general(panel_t, piece_t, (((1,), (1,)), ((), ())), preferred_ele...  10.3 us
    ppermute x9, starting transfers between devices, shifted(): return lax.ppermute(value, axis, pairs)  10.1 us
    all_gather x1, blocking collectives, per_device(): lax.all_gather(own_student, 'narrow', axis=0, tiled=True)  7.95 us
    all_gather x1, blocking collectives, per_device(): lax.all_gather(own_group, 'narrow', axis=0, tiled=True)  5.94 us
  transfers between devices with their start and end apart: 12, of which 8 were waited for; matrix products, arithmetic and copies ran while one was open for 8% of the time, Pallas kernels for 0%

commit v1 on v0

v1 whole, which is shorter than its diff:
```python
import functools

import jax
import jax.numpy as jnp
from jax import lax
from jax.experimental import pallas as pl
from jax.experimental.pallas import tpu as pltpu
from jax.sharding import PartitionSpec as P

AXES = ("wide", "narrow")
NT = (((1,), (1,)), ((), ()))
TN = (((0,), (0,)), ((), ()))


def pair_kernel(block, blocks, mask_ref, rows_ref, all_ref, stud_ref, gcol_ref, grow_ref, out_ref):
    tile = rows_ref.shape[0]
    mine = pl.program_id(0) * tile // block
    rows = rows_ref[...]
    gcol = gcol_ref[...]

    def step(b, acc):
        cols = pl.ds(pl.multiple_of(b * block, block), block)
        e = lax.dot_general(rows, all_ref[cols, :], NT, preferred_element_type=jnp.float32)
        f = mask_ref[mine, b]
        w = jnp.where(gcol == grow_ref[:, cols], 2.0 * f, f)
        p = (e * w).astype(jnp.bfloat16)
        return acc + jnp.dot(p, stud_ref[cols, :], preferred_element_type=jnp.float32)

    acc = lax.fori_loop(
        0, blocks, step, jnp.zeros((tile, stud_ref.shape[1]), jnp.float32), unroll=blocks <= 4
    )
    out_ref[...] = acc.astype(jnp.bfloat16)


def pair_part(mask_sym, columns, student, group, block):
    n, dc = columns.shape
    p = student.shape[1]
    tile = block // 2
    blocks = n // block
    whole = lambda i: (0, 0)
    mine = lambda i: (i, 0)
    return pl.pallas_call(
        functools.partial(pair_kernel, block, blocks),
        grid=(n // tile,),
        in_specs=[
            pl.BlockSpec(memory_space=pltpu.SMEM),
            pl.BlockSpec((tile, dc), mine),
            pl.BlockSpec((n, dc), whole),
            pl.BlockSpec((n, p), whole),
            pl.BlockSpec((tile, 1), mine),
            pl.BlockSpec((1, n), whole),
        ],
        out_specs=pl.BlockSpec((tile, p), mine),
        out_shape=jax.ShapeDtypeStruct((n, p), jnp.bfloat16),
        compiler_params=pltpu.CompilerParams(vmem_limit_bytes=48 * 2**20),
        cost_estimate=pl.CostEstimate(
            flops=2 * n * n * (dc + p), bytes_accessed=2 * n * (dc + 2 * p), transcendentals=0
        ),
    )(mask_sym, columns, columns, student, group.reshape(n, 1), group.reshape(1, n))


def per_device(teacher, weight, block_mask, item_group):
    rows, d = teacher.shape
    width = weight.shape[1]
    wide = lax.axis_size("wide")
    count = wide * lax.axis_size("narrow")
    block = rows * lax.axis_size("narrow")
    n = rows * count
    here = lax.axis_index("wide")
    columns = lax.all_to_all(teacher, AXES, split_axis=1, concat_axis=0, tiled=True)
    group = lax.all_gather(item_group, AXES, axis=0, tiled=True)
    own = jnp.dot(
        teacher, weight.astype(jnp.bfloat16), preferred_element_type=jnp.float32
    ).astype(jnp.bfloat16)
    student = lax.all_gather(own, AXES, axis=0, tiled=True)
    mask = block_mask.astype(jnp.float32)
    mask_sym = mask + mask.T
    mine = lax.dynamic_index_in_dim(mask_sym, here, 0, keepdims=False)
    per_item = jnp.broadcast_to((mine / width)[:, None], (wide, block)).reshape(1, n)
    same = (item_group[:, None] == group[None, :]).astype(jnp.float32)
    stud = lax.dot_general(own, student, NT, preferred_element_type=jnp.float32)
    near = jnp.dot(
        (per_item * (1.0 + same) * stud).astype(jnp.bfloat16),
        student,
        preferred_element_type=jnp.float32,
    )
    far = pair_part(mask_sym * (-1.0 / d), columns, student, group, block)
    far = lax.all_to_all(far.reshape(count, rows, width), AXES, split_axis=0, concat_axis=0, tiled=True)
    total = near + jnp.sum(far.astype(jnp.float32), axis=0)
    grad = (total * (2.0 * d / (n * width))).astype(jnp.bfloat16)
    grad = lax.all_gather(grad, AXES, axis=0, tiled=True)
    return lax.dot_general(columns, grad, TN, preferred_element_type=jnp.float32)


def solution(mesh):
    in_specs = (P(("parts",) + AXES, None), P(), P("parts", None), P(("parts",) + AXES))
    return jax.shard_map(
        per_device,
        mesh=mesh,
        in_specs=in_specs,
        out_specs=P(("parts",) + AXES, None),
        check_vma=False,
    )
```

time: 226 us -> 152 us (0.67)
  waiting for transfers between devices: 156 us -> 75.3 us
  blocking collectives: 13.9 us -> 30.6 us
  matrix products: 20 us -> 6.33 us
  Pallas kernels: 0 us -> 9.25 us
  other arithmetic: 3.27 us -> 0.16 us
  loops' own time: 2.5 us -> 0 us
    reduce_scatter x2 -> x0, waiting for transfers between devices: 86.3 us -> none  [the longest x1 73.2 us: per_device(): lax.psum_scatter(lax.dot_general(teacher, grad_student, (((0,), (0,)), ((...]
    ppermute x9 -> x0, waiting for transfers between devices: 50.3 us -> none  [shifted(): return lax.ppermute(value, axis, pairs)]
    all_gather x1 -> x2, waiting for transfers between devices: 18.5 us -> 52.5 us  [the longest x1 40.3 us: per_device(): grad = lax.all_gather(grad, AXES, axis=0, tiled=True)]
    all_to_all x0 -> x2, waiting for transfers between devices: none -> 22.8 us  [the longest x1 22.8 us: per_device(): lax.all_to_all(far.reshape(count, rows, width), AXES, split_axis=0, conca...]
    all_gather x2 -> x1, blocking collectives: 13.9 us -> 30.6 us  [per_device(): group = lax.all_gather(item_group, AXES, axis=0, tiled=True)]
    dot_general x14 -> x3, matrix products: 20 us -> 6.33 us  [the longest x1 3.27 us: per_device(): jnp.dot(teacher, weight.astype(jnp.bfloat16), preferred_element_type=jnp....]
    all_to_all x0 -> x2, starting transfers between devices: none -> 11.1 us  [the longest x1 7.49 us: per_device(): lax.all_to_all(teacher, AXES, split_axis=1, concat_axis=0, tiled=True)]
    ppermute x9 -> x0, starting transfers between devices: 10.1 us -> none  [shifted(): return lax.ppermute(value, axis, pairs)]
  transfers between devices with their start and end apart: 12 -> 4, of which waited for: 8 -> 3; matrix products, arithmetic and copies ran while one was open for 8% -> 3% of each run, Pallas kernels for 0% -> 0%
where the time goes in v1:
time: 152 us
  waiting for transfers between devices  75.3 us (50%)
  blocking collectives  30.6 us (20%)
  between operations  13.5 us (9%)
  starting transfers between devices  11.2 us (7%)
  Pallas kernels  9.25 us (6%)
  matrix products  6.33 us (4%)
  local copies, waits for them, and re-layouts  5.12 us (3%)
    all_gather x1, waiting for transfers between devices, per_device(): grad = lax.all_gather(grad, AXES, axis=0, tiled=True)  40.3 us
    all_gather x1, blocking collectives, per_device(): group = lax.all_gather(item_group, AXES, axis=0, tiled=True)  30.6 us
    all_to_all x1, waiting for transfers between devices, per_device(): lax.all_to_all(far.reshape(count, rows, width), AXES, split_axis=0, conca...  22.8 us
    all_gather x1, waiting for transfers between devices, per_device(): student = lax.all_gather(own, AXES, axis=0, tiled=True)  12.3 us
    pallas_call x1, Pallas kernels, pair_part(): pl.pallas_call(functools.partial(pair_kernel, block, blocks), grid=(n //...  9.25 us
    all_to_all x1, starting transfers between devices, per_device(): lax.all_to_all(teacher, AXES, split_axis=1, concat_axis=0, tiled=True)  7.49 us
    all_to_all x1, starting transfers between devices, per_device(): lax.all_to_all(far.reshape(count, rows, width), AXES, split_axis=0, conca...  3.65 us
    dot_general x1, matrix products, per_device(): jnp.dot(teacher, weight.astype(jnp.bfloat16), preferred_element_type=jnp....  3.27 us
  transfers between devices with their start and end apart: 4, of which 3 were waited for; matrix products, arithmetic and copies ran while one was open for 3% of the time, Pallas kernels for 0%

profile of v1, /device:TPU:0, one launch (start us, length us, event | category | flops | bytes accessed | tf_op | source)
XLA Modules:
  0.0 151.5 jit_solution(10799246603602221765)
XLA Ops:
  6.5 0.0 copy-start.2
  6.5 2.4 %copy.22 = bf16[16,16,8,256]{3,2,0,1:T(8,128)(2,1)} copy(bf16[16,16,8,256]{3,2,1,0:T(8,128)(2,1)} %bitcast.34) | data formatting | bytes 2097152 | tf_op jit(solution)/shard_map/all_to_all | solution.py:70
  9.0 0.0 copy-start.4
  9.0 0.0 copy-start.5
  9.0 7.5 %all-to-all-start = ((bf16[128,16,256]{2,0,1:T(8,128)(2,1)}), bf16[128,16,256]{2,0,1:T(8,128)(2,1)S(1)}, u32[]{:S(2)}, u32[]{:S(2)}) async-start(bf16[128,16,256]{2,0,1:T(8,128)(2,1)} %bitcast.27), calls=%async_computation | async-start | bytes 2097152 | tf_op jit(solution)/shard_map/all_to_all | solution.py:70
  16.5 0.0 all-gather.4.cloned.1.call-start
  16.5 0.0 copy-done.2
  16.5 3.3 %fusion.7 = bf16[128,256]{1,0:T(8,128)(2,1)} fusion(bf16[128,4096]{1,0:T(8,128)(2,1)S(1)} %copy-done.2, f32[4096,256]{1,0:T(8,128)} %param.5), kind=kOutput, calls=%fused_computation.10 | convolution fusion | flops 269516800 | bytes 5308416 | tf_op jit(solution)/shard_map/dot_general | solution.py:72
  19.8 0.0 all-gather.4.cloned.1.call-update
  19.8 0.0 copy-done.4
  19.8 0.1 copy.14
  19.9 0.1 copy.15
  20.0 0.0 copy-done.5
  20.0 30.6 %all-gather = s32[16,1,128]{2,1,0:T(1,128)S(1)} all-gather(s32[1,1,128]{2,1,0:T(1,128)S(1)} %bitcast.36), channel_id=1, replica_groups=mesh['parts'=2,'wide'=4,'narrow'=4] {'wide','narrow'}, dimensions={0}, use_global_device_ids=true | all-gather | bytes 8704 | tf_op jit(solution)/shard_map/all_gather | solution.py:71
  50.6 0.4 copy.17.gcol_ref
  51.0 0.0 all-to-all-done
  51.0 12.3 %all-gather.4.cloned.1.call-done.stud_ref = bf16[2048,256]{1,0:T(8,128)(2,1)} async-done(((bf16[128,256]{1,0:T(8,128)(2,1)}), bf16[2048,256]{1,0:T(8,128)(2,1)}) %all-gather.4.cloned.1.call-update) | async-done | bytes 1048592 | tf_op jit(solution)/shard_map/all_gather | solution.py:75
  63.3 0.0 copy-start
  63.3 1.2 copy-done
  64.5 0.0 copy-start.1
  64.5 0.0 copy-start.3
  64.5 9.2 %shard_map.46 = bf16[2048,256]{1,0:T(8,128)(2,1)} custom-call(f32[4,4]{1,0:T(4,128)S(1)} %get-tuple-element.5.mask_ref, bf16[2048,256]{1,0:T(8,128)(2,1)S(1)} %bitcast.28, bf16[2048,256]{1,0:T(8,128)(2,1)S(1)} %bitcast.29, bf16[2048,256]{1,0:T(8,128)(2,1)S(1)} %copy-done, s32[2048,1]{1,0:T(8,128)S(1)} %copy.17.gcol_ref, s32[1,2048]{1,0:T(1,128)S(1)} %bitcast.32), custom_call_target="tpu_custom_call" | custom-call | flops 4294967296 | bytes 3145728 | tf_op jit(solution)/shard_map/pallas_call | solution.py:42
  73.8 3.7 %all-to-all-start.1 = ((bf16[16,128,256]{2,1,0:T(8,128)(2,1)}), bf16[16,128,256]{2,1,0:T(8,128)(2,1)S(1)}, u32[]{:S(2)}, u32[]{:S(2)}) async-start(bf16[16,128,256]{2,1,0:T(8,128)(2,1)} %bitcast.8), calls=%async_computation.1 | async-start | bytes 2097152 | tf_op jit(solution)/shard_map/all_to_all | solution.py:88
  77.4 0.0 all-gather.6.cloned.1.call-start
  77.5 0.1 broadcast_bitcast_fusion
  77.6 22.8 %all-to-all-done.1 = bf16[16,128,256]{2,1,0:T(8,128)(2,1)S(1)} async-done(((bf16[16,128,256]{2,1,0:T(8,128)(2,1)}), bf16[16,128,256]{2,1,0:T(8,128)(2,1)S(1)}, u32[]{:S(2)}, u32[]{:S(2)}) %all-to-all-start.1) | async-done | bytes 1048608 | tf_op jit(solution)/shard_map/all_to_all | solution.py:88
  100.3 0.1 convert_reduce_fusion
  100.5 0.0 copy-done.1
  100.5 0.0 copy-done.3
  100.5 1.4 fusion.6
  101.9 0.0 all-gather.6.cloned.1.call-update
  101.9 40.3 %all-gather.6.cloned.1.call-done = bf16[2048,256]{1,0:T(8,128)(2,1)} async-done(((bf16[128,256]{1,0:T(8,128)(2,1)}), bf16[2048,256]{1,0:T(8,128)(2,1)}) %all-gather.6.cloned.1.call-update) | async-done | bytes 1048592 | tf_op jit(solution)/shard_map/all_gather | solution.py:91
  142.1 1.7 %convolution_bitcast_fusion = f32[256,256]{0,1:T(8,128)S(1)} fusion(bf16[2048,256]{1,0:T(8,128)(2,1)} %all-gather.6.cloned.1.call-done, bf16[2048,256]{1,0:T(8,128)(2,1)S(1)} %bitcast.30), kind=kOutput, calls=%fused_computation.6 | convolution fusion | flops 268435456 | bytes 2359296 | tf_op jit(solution)/shard_map/dot_general | solution.py:92
  143.8 0.8 copy.18
  (4 shorter events, 0.0 us)
Async XLA Ops:
  6.5 10.0 %copy-start.2 = (bf16[128,4096]{1,0:T(8,128)(2,1)S(1)}, bf16[128,4096]{1,0:T(8,128)(2,1)}, u32[]{:S(2)}) copy-start(bf16[128,4096]{1,0:T(8,128)(2,1)} %param.4) | copy-start | bytes 3145732
  9.0 10.9 %copy-start.4 = (s32[4,4]{1,0:T(4,128)S(1)}, s32[4,4]{1,0:T(4,128)}, u32[]{:S(2)}) copy-start(s32[4,4]{1,0:T(4,128)} %param.6) | copy-start | bytes 196
  9.0 11.1 %copy-start.5 = (s32[128]{0:T(128)S(1)}, s32[128]{0:T(128)}, u32[]{:S(2)}) copy-start(s32[128]{0:T(128)} %param.7) | copy-start | bytes 1540
  9.0 42.0 %all-to-all-start = ((bf16[128,16,256]{2,0,1:T(8,128)(2,1)}), bf16[128,16,256]{2,0,1:T(8,128)(2,1)S(1)}, u32[]{:S(2)}, u32[]{:S(2)}) async-start(bf16[128,16,256]{2,0,1:T(8,128)(2,1)} %bitcast.27), calls=%async_computation | async-start | bytes 2097152 | tf_op jit(solution)/shard_map/all_to_all | solution.py:70
  16.5 46.8 %all-gather.4.cloned.1.call-start = ((), (), s32[]{:S(2)}) async-start(), calls=%async_computation.2 | async-start | bytes 1114112 | tf_op jit(solution)/shard_map/all_gather | solution.py:75
  63.3 1.2 copy-start
  64.5 36.0 %copy-start.1 = (bf16[2048,256]{1,0:T(8,128)(2,1)S(1)}, bf16[2048,256]{1,0:T(8,128)(2,1)}, u32[]{:S(2)}) copy-start(bf16[2048,256]{1,0:T(8,128)(2,1)} %all-gather.4.cloned.1.call-done.stud_ref) | copy-start | bytes 3145732
  64.5 36.0 %copy-start.3 = (bf16[128,256]{1,0:T(8,128)(2,1)S(1)}, bf16[128,256]{1,0:T(8,128)(2,1)}, u32[]{:S(2)}) copy-start(bf16[128,256]{1,0:T(8,128)(2,1)} %fusion.7) | copy-start | bytes 196612
  73.8 26.6 %all-to-all-start.1 = ((bf16[16,128,256]{2,1,0:T(8,128)(2,1)}), bf16[16,128,256]{2,1,0:T(8,128)(2,1)S(1)}, u32[]{:S(2)}, u32[]{:S(2)}) async-start(bf16[16,128,256]{2,1,0:T(8,128)(2,1)} %bitcast.8), calls=%async_computation.1 | async-start | bytes 2097152 | tf_op jit(solution)/shard_map/all_to_all | solution.py:88
  77.4 64.7 %all-gather.6.cloned.1.call-start = ((), (), s32[]{:S(2)}) async-start(), calls=%async_computation.3 | async-start | bytes 1114112 | tf_op jit(solution)/shard_map/all_gather | solution.py:91
Sparse Core Ops, SparseCore 0:
  19.9 43.3 all-gather.3
  102.0 40.0 all-gather.5

commit v2 on v1

--- a/solution.py
+++ b/solution.py
@@ -59,6 +59,224 @@
     )(mask_sym, columns, columns, student, group.reshape(n, 1), group.reshape(1, n))
 
 
+def ring_kernel(
+    wide, teacher, weight, mask, group, out,
+    cols, stud, groups, far_out, far_in, grads,
+    t_send, t_recv, g_send, g_recv, f_send, f_recv, s_send, s_recv, d_send, d_recv,
+):
+    rows, d = teacher.shape
+    dc = cols.shape[1]
+    count = wide * 4
+    chips = count // 2
+    w, nn = lax.axis_index("wide"), lax.axis_index("narrow")
+    me = w * 4 + nn
+    core = nn % 2
+    chip = me // 2
+
+    def at(i):
+        return pl.ds(pl.multiple_of(i * rows, rows), rows)
+
+    def dev(i):
+        return {"wide": i // 4, "narrow": i % 4}
+
+    def remote(source, target, send, recv, i):
+        return pltpu.make_async_remote_copy(
+            src_ref=source, dst_ref=target, send_sem=send, recv_sem=recv,
+            device_id=dev(i), device_id_type=pl.DeviceIdType.MESH,
+        )
+
+    barrier = pltpu.get_barrier_semaphore()
+
+    @pl.loop(1, count)
+    def _(k):
+        pl.semaphore_signal(
+            barrier, inc=1, device_id=dev((me + k) % count), device_id_type=pl.DeviceIdType.MESH
+        )
+
+    pl.semaphore_wait(barrier, count - 1)
+
+    def column_copy(peer, origin, k):
+        part = pl.ds(pl.multiple_of(peer * dc, dc), dc)
+        return remote(teacher.at[:, part], cols.at[at(origin), :], t_send.at[k], t_recv.at[k], peer)
+
+    def group_copy(peer, origin, k):
+        return remote(group.at[0], groups.at[origin], g_send.at[k], g_recv.at[k], peer)
+
+    @pl.loop(1, count)
+    def _(k):
+        peer = (me + k) % count
+        column_copy(peer, me, k).start()
+        group_copy(peer, me, k).start()
+
+    cols[at(me), :] = teacher[:, pl.ds(pl.multiple_of(me * dc, dc), dc)]
+    groups[me] = group[0]
+
+    step = 512
+
+    def project(c, acc):
+        part = pl.ds(pl.multiple_of(c * step, step), step)
+        return acc + jnp.dot(
+            teacher[:, part],
+            weight[part, :].astype(jnp.bfloat16),
+            preferred_element_type=jnp.float32,
+        )
+
+    own = lax.fori_loop(
+        0, d // step, project, jnp.zeros((rows, stud.shape[1]), jnp.float32)
+    )
+    stud[at(me), :] = own.astype(jnp.bfloat16)
+
+    def gather(buf, send, recv):
+        nx = (nn + 2) % 4
+        nc = nn + 1 - 2 * core
+        ncx = (nc + 2) % 4
+
+        def copy(origin_w, origin_n, slot, to):
+            part = buf.at[at(origin_w * 4 + origin_n), :]
+            return remote(part, part, send.at[slot], recv.at[slot], to)
+
+        sent = []
+
+        def go(*args):
+            c = copy(*args)
+            c.start()
+            sent.append(c)
+
+        a, b, c1, c2 = 0, wide, 2 * wide, 3 * wide
+        for j in range(1, wide):
+            go(w, nn, a + j, (w + j) % wide * 4 + nn)
+        for j in range(wide):
+            ow = (w + wide - j) % wide
+            if j:
+                copy(ow, nn, a + j, me).wait_recv()
+            go(ow, nn, b + j, w * 4 + nx)
+            go(ow, nn, c1 + j, w * 4 + nc)
+        for j in range(wide):
+            ow = (w + wide - j) % wide
+            copy(ow, nx, b + j, me).wait_recv()
+            go(ow, nx, c2 + j, w * 4 + nc)
+        for j in range(wide):
+            ow = (w + wide - j) % wide
+            copy(ow, nc, c1 + j, me).wait_recv()
+            copy(ow, ncx, c2 + j, me).wait_recv()
+        for c in sent:
+            c.wait_send()
+
+    gather(stud, s_send, s_recv)
+
+    @pl.loop(1, count)
+    def _(k):
+        origin = (me + count - k) % count
+        column_copy(me, origin, k).wait_recv()
+        group_copy(me, origin, k).wait_recv()
+
+    def weights(gcol, b, f):
+        return jnp.concatenate(
+            [jnp.where(gcol == groups[b * 4 + i], 2.0 * f, f) for i in range(4)], axis=1
+        )
+
+    def spread(i):
+        return jnp.broadcast_to(groups[i], (rows, rows)).T
+
+    def terms(left, all_rows, gcol, mine, scale):
+        acc = jnp.zeros((left.shape[0], stud.shape[1]), jnp.float32)
+        for b in range(wide):
+            span = pl.ds(b * 4 * rows, 4 * rows)
+            e = lax.dot_general(left, all_rows[span, :], NT, preferred_element_type=jnp.float32)
+            p = (e * weights(gcol, b, mask[mine, b] * scale)).astype(jnp.bfloat16)
+            acc = acc + jnp.dot(p, stud[span, :], preferred_element_type=jnp.float32)
+        return acc
+
+    def far_rows(q):
+        pair = pl.ds(pl.multiple_of(q * 2 * rows, 2 * rows), 2 * rows)
+        gcol = jnp.concatenate([spread(2 * q), spread(2 * q + 1)], axis=0)
+        far_out[pair, :] = terms(cols[pair, :], cols, gcol, q // 2, -1.0 / d).astype(jnp.bfloat16)
+
+    def far_copy(peer, origin, s, r):
+        return remote(far_out.at[at(peer), :], far_in.at[at(origin), :], f_send.at[s], f_recv.at[r], peer)
+
+    partner = me + 1 - 2 * core
+
+    @pl.loop(1, chips + 1)
+    def _(k):
+        q = (chip + k) % chips
+        far_rows(q)
+
+        @pl.when(k < chips)
+        def _():
+            for t in range(2):
+                far_copy(2 * q + t, me, 2 * k + t, 2 * k + core).start()
+
+    far_copy(partner, me, 0, core).start()
+
+    width = stud.shape[1]
+    total = terms(stud[at(me), :], stud, spread(me), w, 1.0 / width)
+    total = total + far_out[at(me), :].astype(jnp.float32)
+    far_copy(me, partner, 0, 1 - core).wait_recv()
+    total = total + far_in[at(partner), :].astype(jnp.float32)
+
+    def collect(k, total):
+        for t in range(2):
+            origin = 2 * ((chip + chips - k) % chips) + t
+            far_copy(me, origin, 2 * k, 2 * k + t).wait_recv()
+            total = total + far_in[at(origin), :].astype(jnp.float32)
+        return total
+
+    total = lax.fori_loop(1, chips, collect, total)
+    grads[at(me), :] = (total * (2.0 * d / (rows * count * width))).astype(jnp.bfloat16)
+    gather(grads, d_send, d_recv)
+    acc = jnp.zeros(out.shape, jnp.float32)
+    for b in range(wide):
+        span = pl.ds(b * 4 * rows, 4 * rows)
+        acc = acc + lax.dot_general(
+            cols[span, :], grads[span, :], TN, preferred_element_type=jnp.float32
+        )
+    out[...] = acc
+
+    @pl.loop(1, count)
+    def _(k):
+        peer = (me + k) % count
+        column_copy(peer, me, k).wait_send()
+        group_copy(peer, me, k).wait_send()
+
+    @pl.loop(1, chips)
+    def _(k):
+        q = (chip + k) % chips
+        for t in range(2):
+            far_copy(2 * q + t, me, 2 * k + t, 2 * k + core).wait_send()
+
+    far_copy(partner, me, 0, core).wait_send()
+
+
+def in_one(teacher, weight, mask_sym, item_group, wide):
+    rows, d = teacher.shape
+    width = weight.shape[1]
+    count = wide * 4
+    n = rows * count
+    dc = d // count
+    vmem = pl.BlockSpec(memory_space=pltpu.VMEM)
+    sem = pltpu.SemaphoreType.DMA
+    return pl.pallas_call(
+        functools.partial(ring_kernel, wide),
+        in_specs=[vmem, vmem, pl.BlockSpec(memory_space=pltpu.SMEM), vmem],
+        out_specs=vmem,
+        out_shape=jax.ShapeDtypeStruct((dc, width), jnp.float32),
+        scratch_shapes=[
+            pltpu.VMEM((n, dc), jnp.bfloat16),
+            pltpu.VMEM((n, width), jnp.bfloat16),
+            pltpu.VMEM((count, 1, rows), jnp.float32),
+            pltpu.VMEM((n, width), jnp.bfloat16),
+            pltpu.VMEM((n, width), jnp.bfloat16),
+            pltpu.VMEM((n, width), jnp.bfloat16),
+        ]
+        + [sem((count,))] * 6
+        + [sem((4 * wide,))] * 4,
+        compiler_params=pltpu.CompilerParams(
+            collective_id=0, has_side_effects=True, vmem_limit_bytes=40 * 2**20
+        ),
+    )(teacher, weight, mask_sym, item_group.astype(jnp.float32).reshape(1, 1, rows))
+
+
 def per_device(teacher, weight, block_mask, item_group):
     rows, d = teacher.shape
     width = weight.shape[1]
@@ -67,14 +285,16 @@
     block = rows * lax.axis_size("narrow")
     n = rows * count
     here = lax.axis_index("wide")
+    mask = block_mask.astype(jnp.float32)
+    mask_sym = mask + mask.T
+    if count == 4 * wide and d % (count * 128) == 0 and rows == 128 and n <= 2048:
+        return in_one(teacher, weight, mask_sym, item_group, wide)
     columns = lax.all_to_all(teacher, AXES, split_axis=1, concat_axis=0, tiled=True)
     group = lax.all_gather(item_group, AXES, axis=0, tiled=True)
     own = jnp.dot(
         teacher, weight.astype(jnp.bfloat16), preferred_element_type=jnp.float32
     ).astype(jnp.bfloat16)
     student = lax.all_gather(own, AXES, axis=0, tiled=True)
-    mask = block_mask.astype(jnp.float32)
-    mask_sym = mask + mask.T
     mine = lax.dynamic_index_in_dim(mask_sym, here, 0, keepdims=False)
     per_item = jnp.broadcast_to((mine / width)[:, None], (wide, block)).reshape(1, n)
     same = (item_group[:, None] == group[None, :]).astype(jnp.float32)

time: 152 us -> 89.8 us (0.59)
  waiting for transfers between devices: 75.3 us -> 0 us
  Pallas kernels: 9.25 us -> 84 us
  blocking collectives: 30.6 us -> 0 us
  between operations: 13.5 us -> 0.01 us
  starting transfers between devices: 11.2 us -> 0 us
  matrix products: 6.33 us -> 0 us
    pallas_call x1, Pallas kernels: 9.25 us -> 84 us  [in_one(): pl.pallas_call(functools.partial(ring_kernel, wide), in_specs=[vmem, vmem...]
    all_gather x2 -> x0, waiting for transfers between devices: 52.5 us -> none  [the longest x1 40.3 us: per_device(): grad = lax.all_gather(grad, AXES, axis=0, tiled=True)]
    all_gather x1 -> x0, blocking collectives: 30.6 us -> none  [per_device(): group = lax.all_gather(item_group, AXES, axis=0, tiled=True)]
    all_to_all x2 -> x0, waiting for transfers between devices: 22.8 us -> none  [the longest x1 22.8 us: per_device(): lax.all_to_all(far.reshape(count, rows, width), AXES, split_axis=0, conca...]
    all_to_all x2 -> x0, starting transfers between devices: 11.1 us -> none  [the longest x1 7.49 us: per_device(): lax.all_to_all(teacher, AXES, split_axis=1, concat_axis=0, tiled=True)]
    dot_general x3 -> x0, matrix products: 6.33 us -> none  [the longest x1 3.27 us: per_device(): jnp.dot(teacher, weight.astype(jnp.bfloat16), preferred_element_type=jnp....]
    unnamed x15 -> x6, local copies, waits for them, and re-layouts: 1.41 us -> 4.88 us
    all_to_all x1 -> x0, local copies, waits for them, and re-layouts: 2.42 us -> none  [per_device(): lax.all_to_all(teacher, AXES, split_axis=1, concat_axis=0, tiled=True)]
  transfers between devices with their start and end apart: 4 -> 0, of which waited for: 3 -> 0; matrix products, arithmetic and copies ran while one was open for 3% -> 0% of each run, Pallas kernels for 0% -> 0%
where the time goes in v2:
time: 89.8 us; the launch traced here: 89.6 us
  Pallas kernels  84 us (94%)
  local copies, waits for them, and re-layouts  4.98 us (6%)
    pallas_call x1, Pallas kernels, in_one(): pl.pallas_call(functools.partial(ring_kernel, wide), in_specs=[vmem, vmem...  84 us
    unnamed x6, local copies, waits for them, and re-layouts  4.88 us

profile of v2, /device:TPU:0, one launch (start us, length us, event | category | flops | bytes accessed | tf_op | source)
XLA Modules:
  0.0 89.6 jit_solution(9132459217565140163)
XLA Ops:
  0.0 0.7 convert_bitcast_fusion.group
  0.7 0.8 copy.5
  1.4 0.1 copy.6
  1.5 0.0 copy-start
  1.5 2.2 %copy-done = f32[4096,256]{1,0:T(8,128)S(1)} copy-done((f32[4096,256]{1,0:T(8,128)S(1)}, f32[4096,256]{1,0:T(8,128)}, u32[]{:S(2)}) %copy-start) | copy-done | bytes 4194328
  3.7 0.0 copy-start.1
  3.7 1.2 %copy-done.1 = bf16[128,4096]{1,0:T(8,128)(2,1)S(1)} copy-done((bf16[128,4096]{1,0:T(8,128)(2,1)S(1)}, bf16[128,4096]{1,0:T(8,128)(2,1)}, u32[]{:S(2)}) %copy-start.1) | copy-done | bytes 1048600
  4.9 84.0 %shard_map.46 = f32[256,256]{1,0:T(8,128)S(1)} custom-call(bf16[128,4096]{1,0:T(8,128)(2,1)S(1)} %copy-done.1, f32[4096,256]{1,0:T(8,128)S(1)} %copy-done, f32[4,4]{1,0:T(4,128)S(1)} %bitcast_add_fusion.mask, f32[1,1,128]{2,1,0:T(1,128)S(1)} %convert_bitcast_fusion.group), custom_call_target="tpu_custom_call" | custom-call | tf_op jit(solution)/shard_map/pallas_call | solution.py:259
  88.9 0.7 copy.8
  (2 shorter events, 0.0 us)
Async XLA Ops:
  1.5 2.2 %copy-start = (f32[4096,256]{1,0:T(8,128)S(1)}, f32[4096,256]{1,0:T(8,128)}, u32[]{:S(2)}) copy-start(f32[4096,256]{1,0:T(8,128)} %weight.1) | copy-start | bytes 12582916
  3.7 1.2 %copy-start.1 = (bf16[128,4096]{1,0:T(8,128)(2,1)S(1)}, bf16[128,4096]{1,0:T(8,128)(2,1)}, u32[]{:S(2)}) copy-start(bf16[128,4096]{1,0:T(8,128)(2,1)} %teacher.1) | copy-start | bytes 3145732

commit v3 on v2

--- a/solution.py
+++ b/solution.py
@@ -60,18 +60,23 @@
 
 
 def ring_kernel(
-    wide, teacher, weight, mask, group, out,
-    cols, stud, groups, far_out, far_in, grads,
-    t_send, t_recv, g_send, g_recv, f_send, f_recv, s_send, s_recv, d_send, d_recv,
+    wide, teacher_hbm, weight_hbm, mask, group, out,
+    teacher, weight, cols, stud, groups, far_out, c_in, x_out, x_in, z_out, z_in, grads,
+    t_send, t_recv, g_send, g_recv, c_send, c_recv, x_send, x_recv, z_send, z_recv,
+    s_send, s_recv, d_send, d_recv, local,
 ):
     rows, d = teacher.shape
+    loads = [
+        pltpu.make_async_copy(teacher_hbm, teacher, local.at[0]),
+        pltpu.make_async_copy(weight_hbm, weight, local.at[1]),
+    ]
+    for load in loads:
+        load.start()
     dc = cols.shape[1]
     count = wide * 4
-    chips = count // 2
     w, nn = lax.axis_index("wide"), lax.axis_index("narrow")
     me = w * 4 + nn
     core = nn % 2
-    chip = me // 2
 
     def at(i):
         return pl.ds(pl.multiple_of(i * rows, rows), rows)
@@ -97,7 +102,7 @@
 
     def column_copy(peer, origin, k):
         part = pl.ds(pl.multiple_of(peer * dc, dc), dc)
-        return remote(teacher.at[:, part], cols.at[at(origin), :], t_send.at[k], t_recv.at[k], peer)
+        return remote(teacher_hbm.at[:, part], cols.at[at(origin), :], t_send.at[k], t_recv.at[k], peer)
 
     def group_copy(peer, origin, k):
         return remote(group.at[0], groups.at[origin], g_send.at[k], g_recv.at[k], peer)
@@ -108,6 +113,8 @@
         column_copy(peer, me, k).start()
         group_copy(peer, me, k).start()
 
+    for load in loads:
+        load.wait()
     cols[at(me), :] = teacher[:, pl.ds(pl.multiple_of(me * dc, dc), dc)]
     groups[me] = group[0]
 
@@ -187,42 +194,70 @@
             acc = acc + jnp.dot(p, stud[span, :], preferred_element_type=jnp.float32)
         return acc
 
-    def far_rows(q):
+    x = nn // 2
+    other = 1 - core
+    width = stud.shape[1]
+    steps = [(j, 1 - x) for j in range(1, wide + 1)] + [(j, x) for j in range(1, wide + 1)]
+
+    def slot(i):
+        return pl.ds(i * rows, rows)
+
+    def half(i, c):
+        return pl.ds(pl.multiple_of((2 * i + c) * rows, rows), rows)
+
+    def core_copy(i):
+        return remote(
+            far_out.at[half(i, other), :], c_in.at[slot(i), :],
+            c_send.at[i], c_recv.at[i], w * 4 + nn + 1 - 2 * core,
+        )
+
+    def x_copy(j):
+        return remote(
+            x_out.at[slot(j - 1), :], x_in.at[slot(j - 1), :],
+            x_send.at[j - 1], x_recv.at[j - 1], w * 4 + (nn + 2) % 4,
+        )
+
+    def z_copy(j):
+        return remote(
+            z_out.at[slot(j - 1), :], z_in.at[slot(j - 1), :],
+            z_send.at[j - 1], z_recv.at[j - 1], (w + j) % wide * 4 + nn,
+        )
+
+    def compute(i):
+        j, to_x = steps[i]
+        q = (w + j) % wide * 2 + to_x
         pair = pl.ds(pl.multiple_of(q * 2 * rows, 2 * rows), 2 * rows)
         gcol = jnp.concatenate([spread(2 * q), spread(2 * q + 1)], axis=0)
-        far_out[pair, :] = terms(cols[pair, :], cols, gcol, q // 2, -1.0 / d).astype(jnp.bfloat16)
-
-    def far_copy(peer, origin, s, r):
-        return remote(far_out.at[at(peer), :], far_in.at[at(origin), :], f_send.at[s], f_recv.at[r], peer)
-
-    partner = me + 1 - 2 * core
-
-    @pl.loop(1, chips + 1)
-    def _(k):
-        q = (chip + k) % chips
-        far_rows(q)
-
-        @pl.when(k < chips)
-        def _():
-            for t in range(2):
-                far_copy(2 * q + t, me, 2 * k + t, 2 * k + core).start()
-
-    far_copy(partner, me, 0, core).start()
-
-    width = stud.shape[1]
+        far_out[pl.ds(2 * i * rows, 2 * rows), :] = terms(
+            cols[pair, :], cols, gcol, q // 2, -1.0 / d
+        ).astype(jnp.bfloat16)
+        core_copy(i).start()
+
+    def finish(i):
+        j, _ = steps[i]
+        core_copy(i).wait_recv()
+        part = far_out[half(i, core), :].astype(jnp.float32)
+        part = part + c_in[slot(i), :].astype(jnp.float32)
+        if i < wide:
+            x_out[slot(j - 1), :] = part.astype(jnp.bfloat16)
+            x_copy(j).start()
+            return None
+        x_copy(j).wait_recv()
+        part = part + x_in[slot(j - 1), :].astype(jnp.float32)
+        if j < wide:
+            z_out[slot(j - 1), :] = part.astype(jnp.bfloat16)
+            z_copy(j).start()
+        return part
+
+    for i in range(2 * wide):
+        compute(i)
+        if i:
+            finish(i - 1)
     total = terms(stud[at(me), :], stud, spread(me), w, 1.0 / width)
-    total = total + far_out[at(me), :].astype(jnp.float32)
-    far_copy(me, partner, 0, 1 - core).wait_recv()
-    total = total + far_in[at(partner), :].astype(jnp.float32)
-
-    def collect(k, total):
-        for t in range(2):
-            origin = 2 * ((chip + chips - k) % chips) + t
-            far_copy(me, origin, 2 * k, 2 * k + t).wait_recv()
-            total = total + far_in[at(origin), :].astype(jnp.float32)
-        return total
-
-    total = lax.fori_loop(1, chips, collect, total)
+    total = total + finish(2 * wide - 1)
+    for j in range(1, wide):
+        z_copy(j).wait_recv()
+        total = total + z_in[slot(j - 1), :].astype(jnp.float32)
     grads[at(me), :] = (total * (2.0 * d / (rows * count * width))).astype(jnp.bfloat16)
     gather(grads, d_send, d_recv)
     acc = jnp.zeros(out.shape, jnp.float32)
@@ -239,13 +274,12 @@
         column_copy(peer, me, k).wait_send()
         group_copy(peer, me, k).wait_send()
 
-    @pl.loop(1, chips)
-    def _(k):
-        q = (chip + k) % chips
-        for t in range(2):
-            far_copy(2 * q + t, me, 2 * k + t, 2 * k + core).wait_send()
-
-    far_copy(partner, me, 0, core).wait_send()
+    for i in range(2 * wide):
+        core_copy(i).wait_send()
+    for j in range(1, wide + 1):
+        x_copy(j).wait_send()
+    for j in range(1, wide):
+        z_copy(j).wait_send()
 
 
 def in_one(teacher, weight, mask_sym, item_group, wide):
@@ -255,22 +289,29 @@
     n = rows * count
     dc = d // count
     vmem = pl.BlockSpec(memory_space=pltpu.VMEM)
+    hbm = pl.BlockSpec(memory_space=pltpu.HBM)
     sem = pltpu.SemaphoreType.DMA
     return pl.pallas_call(
         functools.partial(ring_kernel, wide),
-        in_specs=[vmem, vmem, pl.BlockSpec(memory_space=pltpu.SMEM), vmem],
+        in_specs=[hbm, hbm, pl.BlockSpec(memory_space=pltpu.SMEM), vmem],
         out_specs=vmem,
         out_shape=jax.ShapeDtypeStruct((dc, width), jnp.float32),
         scratch_shapes=[
+            pltpu.VMEM((rows, d), jnp.bfloat16),
+            pltpu.VMEM((d, width), jnp.float32),
             pltpu.VMEM((n, dc), jnp.bfloat16),
             pltpu.VMEM((n, width), jnp.bfloat16),
             pltpu.VMEM((count, 1, rows), jnp.float32),
             pltpu.VMEM((n, width), jnp.bfloat16),
-            pltpu.VMEM((n, width), jnp.bfloat16),
-            pltpu.VMEM((n, width), jnp.bfloat16),
+            pltpu.VMEM((2 * wide * rows, width), jnp.bfloat16),
         ]
-        + [sem((count,))] * 6
-        + [sem((4 * wide,))] * 4,
+        + [pltpu.VMEM((wide * rows, width), jnp.bfloat16)] * 4
+        + [pltpu.VMEM((n, width), jnp.bfloat16)]
+        + [sem((count,))] * 4
+        + [sem((2 * wide,))] * 2
+        + [sem((wide,))] * 4
+        + [sem((4 * wide,))] * 4
+        + [sem((2,))],
         compiler_params=pltpu.CompilerParams(
             collective_id=0, has_side_effects=True, vmem_limit_bytes=40 * 2**20
         ),

time: 89.8 us -> 76.5 us (0.85); the launches traced: 89.6 us -> 75.3 us
  Pallas kernels: 84 us -> 69.7 us
    pallas_call x1, Pallas kernels: 84 us -> 69.7 us  [in_one(): pl.pallas_call(functools.partial(ring_kernel, wide), in_specs=[hbm, hbm,...]
where the time goes in v3:
time: 76.5 us; the launch traced here: 75.3 us
  Pallas kernels  69.7 us (91%)
  local copies, waits for them, and re-layouts  4.98 us (7%)
    pallas_call x1, Pallas kernels, in_one(): pl.pallas_call(functools.partial(ring_kernel, wide), in_specs=[hbm, hbm,...  69.7 us
    unnamed x6, local copies, waits for them, and re-layouts  4.88 us

profile of v3, /device:TPU:0, one launch (start us, length us, event | category | flops | bytes accessed | tf_op | source)
XLA Modules:
  0.0 75.3 jit_solution(13768465364372767042)
XLA Ops:
  0.0 0.7 convert_bitcast_fusion.group
  0.7 0.8 %copy.5 = s32[4,4]{0,1:T(4,128)S(1)} copy(s32[4,4]{1,0:T(4,128)} %param.6) | data formatting | bytes 128 | tf_op args[2]
  1.4 0.1 copy.6
  1.5 0.0 copy-start
  1.5 2.2 %copy-done = f32[4096,256]{1,0:T(8,128)S(1)} copy-done((f32[4096,256]{1,0:T(8,128)S(1)}, f32[4096,256]{1,0:T(8,128)}, u32[]{:S(2)}) %copy-start) | copy-done | bytes 4194328
  3.7 0.0 copy-start.1
  3.7 1.2 %copy-done.1 = bf16[128,4096]{1,0:T(8,128)(2,1)S(1)} copy-done((bf16[128,4096]{1,0:T(8,128)(2,1)S(1)}, bf16[128,4096]{1,0:T(8,128)(2,1)}, u32[]{:S(2)}) %copy-start.1) | copy-done | bytes 1048600
  4.9 69.7 %shard_map.46 = f32[256,256]{1,0:T(8,128)S(1)} custom-call(bf16[128,4096]{1,0:T(8,128)(2,1)S(1)} %copy-done.1, f32[4096,256]{1,0:T(8,128)S(1)} %copy-done, f32[4,4]{1,0:T(4,128)S(1)} %bitcast_add_fusion.mask, f32[1,1,128]{2,1,0:T(1,128)S(1)} %convert_bitcast_fusion.group), custom_call_target="tpu_custom_call" | custom-call | tf_op jit(solution)/shard_map/pallas_call | solution.py:294
  74.6 0.7 copy.8
  (2 shorter events, 0.0 us)
Async XLA Ops:
  1.5 2.2 %copy-start = (f32[4096,256]{1,0:T(8,128)S(1)}, f32[4096,256]{1,0:T(8,128)}, u32[]{:S(2)}) copy-start(f32[4096,256]{1,0:T(8,128)} %weight_hbm.1) | copy-start | bytes 12582916
  3.7 1.2 %copy-start.1 = (bf16[128,4096]{1,0:T(8,128)(2,1)S(1)}, bf16[128,4096]{1,0:T(8,128)(2,1)}, u32[]{:S(2)}) copy-start(bf16[128,4096]{1,0:T(8,128)(2,1)} %teacher_hbm.1) | copy-start | bytes 3145732

commit v4 on v3

--- a/solution.py
+++ b/solution.py
@@ -61,7 +61,7 @@
 
 def ring_kernel(
     wide, teacher_hbm, weight_hbm, mask, group, out,
-    teacher, weight, cols, stud, groups, far_out, c_in, x_out, x_in, z_out, z_in, grads,
+    teacher, weight, cols, stud, groups, far_out, c_in, x_out, x_in, z_out, z_in, grads, flipped,
     t_send, t_recv, g_send, g_recv, c_send, c_recv, x_send, x_recv, z_send, z_recv,
     s_send, s_recv, d_send, d_recv, local,
 ):
@@ -133,7 +133,7 @@
     )
     stud[at(me), :] = own.astype(jnp.bfloat16)
 
-    def gather(buf, send, recv):
+    def gather(buf, send, recv, use):
         nx = (nn + 2) % 4
         nc = nn + 1 - 2 * core
         ncx = (nc + 2) % 4
@@ -149,27 +149,36 @@
             c.start()
             sent.append(c)
 
+        def landed(*args):
+            copy(*args, me).wait_recv()
+
         a, b, c1, c2 = 0, wide, 2 * wide, 3 * wide
+        planes = [w, w + 1 - 2 * (w % 2), (w + 2) % 4, 3 - w]
+        for j in (3, 2, 1):
+            go(w, nn, a + j, planes[j] * 4 + nn)
+        go(w, nn, b, w * 4 + nx)
+        go(w, nn, c1, w * 4 + nc)
+        landed(w, nx, b)
+        go(w, nx, c2, w * 4 + nc)
         for j in range(1, wide):
-            go(w, nn, a + j, (w + j) % wide * 4 + nn)
-        for j in range(wide):
-            ow = (w + wide - j) % wide
-            if j:
-                copy(ow, nn, a + j, me).wait_recv()
-            go(ow, nn, b + j, w * 4 + nx)
-            go(ow, nn, c1 + j, w * 4 + nc)
-        for j in range(wide):
-            ow = (w + wide - j) % wide
-            copy(ow, nx, b + j, me).wait_recv()
-            go(ow, nx, c2 + j, w * 4 + nc)
-        for j in range(wide):
-            ow = (w + wide - j) % wide
-            copy(ow, nc, c1 + j, me).wait_recv()
-            copy(ow, ncx, c2 + j, me).wait_recv()
+            landed(planes[j], nn, a + j)
+            go(planes[j], nn, b + j, w * 4 + nx)
+            go(planes[j], nn, c1 + j, w * 4 + nc)
+            if j == 1:
+                landed(w, nc, c1)
+                landed(w, ncx, c2)
+                use(w)
+        for j in range(1, wide):
+            landed(planes[j], nx, b + j)
+            go(planes[j], nx, c2 + j, w * 4 + nc)
+        for j in range(1, wide):
+            landed(planes[j], nc, c1 + j)
+            landed(planes[j], ncx, c2 + j)
+            use(planes[j])
         for c in sent:
             c.wait_send()
 
-    gather(stud, s_send, s_recv)
+    gather(stud, s_send, s_recv, lambda plane: None)
 
     @pl.loop(1, count)
     def _(k):
@@ -179,18 +188,19 @@
 
     def weights(gcol, b, f):
         return jnp.concatenate(
-            [jnp.where(gcol == groups[b * 4 + i], 2.0 * f, f) for i in range(4)], axis=1
+            [jnp.where(gcol == groups[b * 4 + i].astype(jnp.float32), 2.0 * f, f) for i in range(4)], axis=1
         )
 
     def spread(i):
-        return jnp.broadcast_to(groups[i], (rows, rows)).T
+        return jnp.broadcast_to(groups[i].astype(jnp.float32), (rows, rows)).T
 
     def terms(left, all_rows, gcol, mine, scale):
         acc = jnp.zeros((left.shape[0], stud.shape[1]), jnp.float32)
         for b in range(wide):
             span = pl.ds(b * 4 * rows, 4 * rows)
             e = lax.dot_general(left, all_rows[span, :], NT, preferred_element_type=jnp.float32)
-            p = (e * weights(gcol, b, mask[mine, b] * scale)).astype(jnp.bfloat16)
+            f = (mask[mine, b] + mask[b, mine]).astype(jnp.float32) * scale
+            p = (e * weights(gcol, b, f)).astype(jnp.bfloat16)
             acc = acc + jnp.dot(p, stud[span, :], preferred_element_type=jnp.float32)
         return acc
 
@@ -255,18 +265,20 @@
             finish(i - 1)
     total = terms(stud[at(me), :], stud, spread(me), w, 1.0 / width)
     total = total + finish(2 * wide - 1)
+    for b in range(wide):
+        span = pl.ds(b * 4 * rows, 4 * rows)
+        flipped[:, span] = cols[span, :].T
     for j in range(1, wide):
         z_copy(j).wait_recv()
         total = total + z_in[slot(j - 1), :].astype(jnp.float32)
     grads[at(me), :] = (total * (2.0 * d / (rows * count * width))).astype(jnp.bfloat16)
-    gather(grads, d_send, d_recv)
-    acc = jnp.zeros(out.shape, jnp.float32)
-    for b in range(wide):
-        span = pl.ds(b * 4 * rows, 4 * rows)
-        acc = acc + lax.dot_general(
-            cols[span, :], grads[span, :], TN, preferred_element_type=jnp.float32
-        )
-    out[...] = acc
+    out[...] = jnp.zeros_like(out)
+
+    def use(plane):
+        span = pl.ds(pl.multiple_of(plane * 4 * rows, 4 * rows), 4 * rows)
+        out[...] += jnp.dot(flipped[:, span], grads[span, :], preferred_element_type=jnp.float32)
+
+    gather(grads, d_send, d_recv, use)
 
     @pl.loop(1, count)
     def _(k):
@@ -282,7 +294,7 @@
         z_copy(j).wait_send()
 
 
-def in_one(teacher, weight, mask_sym, item_group, wide):
+def in_one(teacher, weight, block_mask, item_group, wide):
     rows, d = teacher.shape
     width = weight.shape[1]
     count = wide * 4
@@ -301,21 +313,21 @@
             pltpu.VMEM((d, width), jnp.float32),
             pltpu.VMEM((n, dc), jnp.bfloat16),
             pltpu.VMEM((n, width), jnp.bfloat16),
-            pltpu.VMEM((count, 1, rows), jnp.float32),
+            pltpu.VMEM((count, 1, rows), jnp.int32),
             pltpu.VMEM((n, width), jnp.bfloat16),
             pltpu.VMEM((2 * wide * rows, width), jnp.bfloat16),
         ]
         + [pltpu.VMEM((wide * rows, width), jnp.bfloat16)] * 4
-        + [pltpu.VMEM((n, width), jnp.bfloat16)]
+        + [pltpu.VMEM((n, width), jnp.bfloat16), pltpu.VMEM((dc, n), jnp.bfloat16)]
         + [sem((count,))] * 4
         + [sem((2 * wide,))] * 2
         + [sem((wide,))] * 4
         + [sem((4 * wide,))] * 4
         + [sem((2,))],
         compiler_params=pltpu.CompilerParams(
-            collective_id=0, has_side_effects=True, vmem_limit_bytes=40 * 2**20
+            collective_id=0, has_side_effects=True, vmem_limit_bytes=62 * 2**20
         ),
-    )(teacher, weight, mask_sym, item_group.astype(jnp.float32).reshape(1, 1, rows))
+    )(teacher, weight, block_mask, item_group.reshape(1, 1, rows))
 
 
 def per_device(teacher, weight, block_mask, item_group):
@@ -328,8 +340,8 @@
     here = lax.axis_index("wide")
     mask = block_mask.astype(jnp.float32)
     mask_sym = mask + mask.T
-    if count == 4 * wide and d % (count * 128) == 0 and rows == 128 and n <= 2048:
-        return in_one(teacher, weight, mask_sym, item_group, wide)
+    if count == 4 * wide and wide == 4 and d % (count * 128) == 0 and rows == 128 and n <= 2048:
+        return in_one(teacher, weight, block_mask, item_group, wide)
     columns = lax.all_to_all(teacher, AXES, split_axis=1, concat_axis=0, tiled=True)
     group = lax.all_gather(item_group, AXES, axis=0, tiled=True)
     own = jnp.dot(

time: 76.5 us -> 72.1 us (0.942); the launches traced: 75.3 us -> 71.8 us
  local copies, waits for them, and re-layouts: 4.98 us -> 1.67 us
    unnamed x6 -> x1, local copies, waits for them, and re-layouts: 4.88 us -> 1.67 us
where the time goes in v4:
time: 72.1 us; the launch traced here: 71.8 us
  Pallas kernels  70.1 us (97%)
  local copies, waits for them, and re-layouts  1.67 us (2%)
    pallas_call x1, Pallas kernels, in_one(): pl.pallas_call(functools.partial(ring_kernel, wide), in_specs=[hbm, hbm,...  70.1 us
    unnamed x1, local copies, waits for them, and re-layouts  1.67 us

profile of v4, /device:TPU:0, one launch (start us, length us, event | category | flops | bytes accessed | tf_op | source)
XLA Modules:
  0.0 71.8 jit_solution(204621246803888969)
XLA Ops:
  0.0 70.1 %shard_map.46 = f32[256,256]{1,0:T(8,128)} custom-call(bf16[128,4096]{1,0:T(8,128)(2,1)} %teacher_hbm.1, f32[4096,256]{1,0:T(8,128)} %weight_hbm.1, s32[4,4]{1,0:T(4,128)} %mask.1, s32[1,1,128]{2,1,0:T(1,128)} %bitcast.1), custom_call_target="tpu_custom_call" | custom-call | tf_op jit(solution)/shard_map/pallas_call | solution.py:306
  70.1 1.7 %copy.6 = f32[256,256]{1,0:T(8,128)} copy(f32[256,256]{1,0:T(8,128)} %shard_map.46) | data formatting | bytes 524288

commit v5 on v4

--- a/solution.py
+++ b/solution.py
@@ -109,9 +109,15 @@
 
     @pl.loop(1, count)
     def _(k):
-        peer = (me + k) % count
-        column_copy(peer, me, k).start()
-        group_copy(peer, me, k).start()
+        group_copy((me + k) % count, me, k).start()
+
+    def send_columns(first, last):
+        @pl.loop(first, last)
+        def _(i):
+            k = 1 + (i + 6) % (count - 1)
+            column_copy((me + k) % count, me, k).start()
+
+    send_columns(0, 5)
 
     for load in loads:
         load.wait()
@@ -133,7 +139,7 @@
     )
     stud[at(me), :] = own.astype(jnp.bfloat16)
 
-    def gather(buf, send, recv, use):
+    def gather(buf, send, recv, use, then):
         nx = (nn + 2) % 4
         nc = nn + 1 - 2 * core
         ncx = (nc + 2) % 4
@@ -158,6 +164,7 @@
             go(w, nn, a + j, planes[j] * 4 + nn)
         go(w, nn, b, w * 4 + nx)
         go(w, nn, c1, w * 4 + nc)
+        then()
         landed(w, nx, b)
         go(w, nx, c2, w * 4 + nc)
         for j in range(1, wide):
@@ -178,7 +185,7 @@
         for c in sent:
             c.wait_send()
 
-    gather(stud, s_send, s_recv, lambda plane: None)
+    gather(stud, s_send, s_recv, lambda plane: None, lambda: send_columns(5, count - 1))
 
     @pl.loop(1, count)
     def _(k):
@@ -278,7 +285,7 @@
         span = pl.ds(pl.multiple_of(plane * 4 * rows, 4 * rows), 4 * rows)
         out[...] += jnp.dot(flipped[:, span], grads[span, :], preferred_element_type=jnp.float32)
 
-    gather(grads, d_send, d_recv, use)
+    gather(grads, d_send, d_recv, use, lambda: None)
 
     @pl.loop(1, count)
     def _(k):

time: 72.1 us -> 67.9 us (0.942)
  Pallas kernels: 70.1 us -> 65.9 us
    pallas_call x1, Pallas kernels: 70.1 us -> 65.9 us  [in_one(): pl.pallas_call(functools.partial(ring_kernel, wide), in_specs=[hbm, hbm,...]
where the time goes in v5:
time: 67.9 us; the launch traced here: 67.6 us
  Pallas kernels  65.9 us (97%)
  local copies, waits for them, and re-layouts  1.67 us (2%)
    pallas_call x1, Pallas kernels, in_one(): pl.pallas_call(functools.partial(ring_kernel, wide), in_specs=[hbm, hbm,...  65.9 us
    unnamed x1, local copies, waits for them, and re-layouts  1.67 us

profile of v5, /device:TPU:0, one launch (start us, length us, event | category | flops | bytes accessed | tf_op | source)
XLA Modules:
  0.0 67.6 jit_solution(14843092031917640767)
XLA Ops:
  0.0 65.9 %shard_map.46 = f32[256,256]{1,0:T(8,128)} custom-call(bf16[128,4096]{1,0:T(8,128)(2,1)} %teacher_hbm.1, f32[4096,256]{1,0:T(8,128)} %weight_hbm.1, s32[4,4]{1,0:T(4,128)} %mask.1, s32[1,1,128]{2,1,0:T(1,128)} %bitcast.1), custom_call_target="tpu_custom_call" | custom-call | tf_op jit(solution)/shard_map/pallas_call | solution.py:313
  65.9 1.7 %copy.6 = f32[256,256]{1,0:T(8,128)} copy(f32[256,256]{1,0:T(8,128)} %shard_map.46) | data formatting | bytes 524288

commit v6 on v5

--- a/solution.py
+++ b/solution.py
@@ -185,7 +185,12 @@
         for c in sent:
             c.wait_send()
 
-    gather(stud, s_send, s_recv, lambda plane: None, lambda: send_columns(5, count - 1))
+    def send_rest():
+        send_columns(5, 9)
+        send_columns(12, count - 1)
+        send_columns(9, 12)
+
+    gather(stud, s_send, s_recv, lambda plane: None, send_rest)
 
     @pl.loop(1, count)
     def _(k):
@@ -214,7 +219,7 @@
     x = nn // 2
     other = 1 - core
     width = stud.shape[1]
-    steps = [(j, 1 - x) for j in range(1, wide + 1)] + [(j, x) for j in range(1, wide + 1)]
+    steps = [(j, 1 - x) for j in (2, 1, 3, 4)] + [(j, x) for j in (2, 1, 3, 4)]
 
     def slot(i):
         return pl.ds(i * rows, rows)

time: 67.9 us -> 67.9 us (level)
  no operation moved by 1% of the time
where the time goes in v6:
time: 67.9 us; the launch traced here: 67.5 us
  Pallas kernels  65.8 us (97%)
  local copies, waits for them, and re-layouts  1.67 us (2%)
    pallas_call x1, Pallas kernels, in_one(): pl.pallas_call(functools.partial(ring_kernel, wide), in_specs=[hbm, hbm,...  65.8 us
    unnamed x1, local copies, waits for them, and re-layouts  1.67 us

profile of v6, /device:TPU:0, one launch (start us, length us, event | category | flops | bytes accessed | tf_op | source)
XLA Modules:
  0.0 67.5 jit_solution(10001741199558994189)
XLA Ops:
  0.0 65.8 %shard_map.46 = f32[256,256]{1,0:T(8,128)} custom-call(bf16[128,4096]{1,0:T(8,128)(2,1)} %teacher_hbm.1, f32[4096,256]{1,0:T(8,128)} %weight_hbm.1, s32[4,4]{1,0:T(4,128)} %mask.1, s32[1,1,128]{2,1,0:T(1,128)} %bitcast.1), custom_call_target="tpu_custom_call" | custom-call | tf_op jit(solution)/shard_map/pallas_call | solution.py:318
  65.8 1.7 %copy.6 = f32[256,256]{1,0:T(8,128)} copy(f32[256,256]{1,0:T(8,128)} %shard_map.46) | data formatting | bytes 524288
